TPU v7x, 32 devices: a whole 2x2x4 slice. The times are simulated.
32 devices in a mesh: leaf: 32 (over z, y, x, core).
Axes of the slice: x: 2, y: 2, z: 4, core: 2. Of those that a mesh axis runs over, the one named last changes fastest.
Arguments:
- points: bfloat16 [65536, 128], P('leaf'), may hold values from -6 to 6
- charges: bfloat16 [65536, 256], P('leaf'), may hold values from -6 to 6
- order: int32 [32, 2048], P('leaf'), may hold values from 0 to 2047, each once within a row
- near: int32 [32, 2], P('leaf'), may hold values from 0 to 31, as said below
- bases: bfloat16 [65536, 256], P('leaf'), may hold values from -0.125 to 0.125
- lift_leaf: float32 [8192, 256], P('leaf'), may hold values from -0.1875 to 0.1875
- lift_node: float32 [2048, 256], P('leaf'), may hold values from -0.1875 to 0.1875
- proxy_leaf: float32 [8192, 128], P('leaf'), may hold values from -5 to 5
- proxy_node: float32 [2048, 128], P('leaf'), may hold values from -5 to 5
- proxy_top: float32 [512, 128], P('leaf'), may hold values from -5 to 5
Outputs:
- potential: bfloat16 [65536, 256], P('leaf')
Inputs may be any that keep to these rules, and one draw needn't show every extreme that they name: `order`: each row is a permutation of the leaf's 2048 positions. `near`: row l names two distinct leaves other than l from l's aligned group of four leaves; the relation is symmetric, and the group's remaining leaf is l's far partner, whose index differs from l in exactly one of the two lowest bits.
All inputs are finite; a program needn't handle non-finite values.
Results may differ from a plain program's by a relative error of at most 0.0049.
Values may be sent and summed in bfloat16 or wider, within the bound.
A program may use at most 64 MiB of HBM per device.

v0:
```python
import functools

import jax
import jax.numpy as jnp
from jax import lax
from jax.experimental import pallas as pl
from jax.experimental.pallas import tpu as pltpu
from jax.sharding import PartitionSpec as P

MESH = pl.DeviceIdType.MESH
F32, BF16 = jnp.float32, jnp.bfloat16
CHUNKS = 8
EARLY = 6
ROWS = 1024


def mm(a, b, ca=1, cb=0):
    return lax.dot_general(a, b, (((ca,), (cb,)), ((), ())), preferred_element_type=F32)


def split3(x):
    high = x.astype(BF16).astype(F32)
    middle = (x - high).astype(BF16).astype(F32)
    return high, middle, x - high - middle


def norm_column(p):
    wide = p.astype(F32)
    return jnp.sum(wide * wide, axis=1, keepdims=True)


def norm_lanes(p, one_scale, norm_scale, norm_first):
    high, middle, low = split3(norm_column(p))
    lane = lax.broadcasted_iota(jnp.int32, (p.shape[0], 128), 1)
    first = 0 if norm_first else 3
    ones = jnp.where(lane < 6, one_scale, 0.0)
    out = jnp.where(lane == first, high * norm_scale, ones)
    out = jnp.where(lane == first + 1, middle * norm_scale, out)
    out = jnp.where(lane == first + 2, low * norm_scale, out)
    return out.astype(BF16)


def couple(left, right):
    scale = 2.0 / left.shape[1]
    wide = right.astype(F32)
    square = wide * wide
    high = square.astype(BF16)
    low = (square - high.astype(F32)).astype(BF16)
    ones = jnp.ones((8, left.shape[1]), BF16)
    right_norm = (mm(ones, high, 1, 1) + mm(ones, low, 1, 1))[0:1, :]
    return jnp.exp((2.0 * mm(left, right, 1, 1) - norm_column(left) - right_norm) * scale).astype(BF16)


def kernel(n, near, points_in, charges_in, bases_in, order, lift, nlift, zleaf, znode, ztop, out,
           points, charges, bases, rhs, laug, raug, acc, p1, p2, p3, r1, r2, r3, cp, cr,
           c0, c0x, z0, z0x, ut, us, rs, nl, z1, z1s, z2, nv, nvs, c2, c2o, z2o, f1,
           ssem, rsem, lsem):
    me = lax.axis_index("leaf")
    leaf, dim = points.shape
    rank = lift.shape[0]
    quarter = rank // 4
    head = leaf * 3 // 4
    sixteenth = rank // 16
    nodes = n // 16
    slot = me % 4
    group = me // 4 % 4
    part = me % 16
    node = me // 16
    step = leaf // CHUNKS

    def flip(bits):
        if bits == 1:
            return me + 1 - 2 * (me % 2)
        if bits == 2:
            return me + 2 - 4 * (me // 2 % 2)
        if bits == 3:
            return me - slot + 3 - slot
        if bits == 4:
            return me + 4 - 8 * (me // 4 % 2)
        if bits == 8:
            return me + 8 - 16 * (me // 8 % 2)
        return me - 4 * group + 4 * (3 - group)

    def flip_slot(bits):
        if bits == 1:
            return slot + 1 - 2 * (slot % 2)
        if bits == 2:
            return slot + 2 - 4 * (slot // 2)
        return 3 - slot

    others = [(node + d) % nodes * 16 + part for d in range(1, nodes)]

    barrier = pltpu.get_barrier_semaphore()
    partners = [flip(b) for b in (1, 2, 3, 4, 8, 12)] + others
    for other in partners:
        pl.semaphore_signal(barrier, inc=1, device_id=(other,), device_id_type=MESH)

    loads = [pltpu.make_async_copy(a, b, lsem.at[i]) for i, (a, b) in enumerate(
        ((charges_in, charges), (bases_in, bases), (points_in, points)))]
    for copy in loads:
        copy.start()
    count = [0]
    started = []

    def send(src, dst, device):
        i = count[0]
        count[0] += 1
        copy = pltpu.make_async_remote_copy(
            src_ref=src, dst_ref=dst, send_sem=ssem.at[i], recv_sem=rsem.at[i],
            device_id=(device,), device_id_type=MESH)
        copy.start()
        started.append(copy)
        return copy

    mine = pl.ds(pl.multiple_of(slot * quarter, quarter), quarter)
    mine16 = pl.ds(pl.multiple_of(part * sixteenth, sixteenth), sixteenth)
    mine64 = pl.ds(pl.multiple_of(group * quarter, quarter), quarter)
    z1[mine, :] = znode[...].astype(BF16)
    nl[mine, :] = nlift[...].astype(BF16)
    z2[mine16, :] = ztop[...].astype(BF16)
    z0[...] = zleaf[...].astype(BF16)
    pl.semaphore_wait(barrier, len(partners))

    def at_slot(bits):
        where = flip_slot(bits) if bits else slot
        return pl.ds(pl.multiple_of(where * quarter, quarter), quarter)

    far16 = pl.ds(pl.multiple_of(flip(2) % 16 * sixteenth, sixteenth), sixteenth)
    phase_a2 = [send(z1.at[mine, :], z1.at[mine, :], flip(2)),
                send(nl.at[mine, :], nl.at[mine, :], flip(2)),
                send(z2.at[mine16, :], z2.at[mine16, :], flip(2))]
    top, rest = pl.ds(0, head), pl.ds(head, leaf - head)
    points_two = send(points_in.at[top, :], p2.at[top, :], flip(2))
    phase_a = [send(z1.at[mine, :], z1.at[mine, :], flip(1)),
               send(nl.at[mine, :], nl.at[mine, :], flip(1)),
               send(z2.at[mine16, :], z2.at[mine16, :], flip(1))]
    points_one = send(points_in, p1, flip(1))
    loads[0].wait()

    def permute(block, carry):
        rows = pl.ds(pl.multiple_of(block * 128, 128), 128)
        index = jnp.broadcast_to(order[0:1, rows].astype(F32), (128, 128)).T
        lane = lax.broadcasted_iota(jnp.int32, (128, 128), 1).astype(F32)
        chosen = jnp.concatenate(
            [jnp.where(index == lane + 128.0 * j, 1.0, 0.0).astype(BF16) for j in range(leaf // 128)], 1)
        rhs[rows, :] = mm(chosen, charges[...]).astype(BF16)
        return carry

    lax.fori_loop(0, leaf // 128, permute, 0)

    loads[1].wait()
    own = mm(rhs[...], bases[...], 0, 0).astype(BF16)
    c0[...] = own
    up = mm(own, lift[...].astype(BF16))
    ut[...] = up.astype(BF16)
    up_near = send(ut.at[at_slot(1), :], rs.at[0], flip(1))
    up_cross = send(ut.at[at_slot(3), :], rs.at[1], flip(1))
    rhs_one = send(rhs, r1, flip(1))
    for copy in phase_a2:
        copy.wait_recv()
    phase_a.append(send(z1.at[at_slot(2), :], z1.at[at_slot(2), :], flip(1)))
    phase_a.append(send(nl.at[at_slot(2), :], nl.at[at_slot(2), :], flip(1)))
    phase_a.append(send(z2.at[far16, :], z2.at[far16, :], flip(1)))
    rhs_two = []

    def send_chunk(c):
        rows = pl.ds(c * step, step)
        rhs_two.append(send(rhs.at[rows, :], r2.at[rows, :], flip(2)))

    loads[2].wait()
    up_cross.wait_recv()
    us[...] = (ut[at_slot(2), :].astype(F32) + rs[1].astype(F32)).astype(BF16)
    up_two = send(us, rs.at[2], flip(2))
    points_rest = send(points_in.at[rest, :], p2.at[rest, :], flip(2))
    send_chunk(0)
    send_chunk(1)
    phase_far = []
    for b in (1, 2):
        phase_far.append(send(c0, c0x.at[b - 1], flip(b)))
        phase_far.append(send(z0, z0x.at[b - 1], flip(b)))
    for c in range(2, EARLY):
        send_chunk(c)

    def augment(block, carry):
        rows = pl.ds(pl.multiple_of(block * ROWS, ROWS), ROWS)
        p = points[rows, :]
        laug[rows, 0:dim] = (p.astype(F32) * (4.0 / dim)).astype(BF16)
        laug[rows, dim:] = norm_lanes(p, -2.0 / dim, -2.0 / dim, False)
        raug[rows, 0:dim] = p
        raug[rows, dim:] = norm_lanes(p, 1.0, 1.0, True)
        return carry

    lax.fori_loop(0, leaf // ROWS, augment, 0)

    def tiles(rows, right, width):
        left = laug[rows, :]
        return jnp.concatenate(
            [jnp.exp(mm(left, right[j:j + 512, :], 1, 1)).astype(BF16) for j in range(0, width, 512)], 1)

    def own_tile(block, carry):
        rows = pl.ds(pl.multiple_of(block * ROWS, ROWS), ROWS)
        acc[rows, :] = mm(tiles(rows, raug, leaf), rhs[...])
        return carry

    blocks = leaf // ROWS
    for copy in phase_a:
        copy.wait_recv()
    phase_b = []
    for i, b in enumerate((4, 8, 12)):
        phase_b.append(send(z1, z1s.at[i], flip(b)))
        phase_b.append(send(z2.at[mine64, :], z2.at[mine64, :], flip(b)))

    lax.fori_loop(0, blocks // 2, own_tile, 0)

    up_near.wait_recv()
    up_two.wait_recv()
    total = ut[mine, :].astype(F32) + rs[0].astype(F32) + rs[2].astype(F32)
    nv[0] = total.astype(BF16)
    lifted = mm(total.astype(BF16), nl[...])
    nv[1] = lifted.astype(BF16)
    phase_two = [send(nv, nvs.at[i], flip(b)) for i, b in enumerate((4, 8, 12))]
    points_two.wait_recv()
    points_three = [send(p2.at[top, :], p3.at[top, :], flip(1))]

    lax.fori_loop(blocks // 2, blocks, own_tile, 0)

    for copy in phase_b:
        copy.wait_recv()
    for copy in phase_two:
        copy.wait_recv()
    for i in range(3):
        lifted = lifted + nvs[i, 1].astype(F32)
    c2[...] = lifted.astype(BF16)
    phase_top = []
    for d, other in enumerate(others):
        phase_top.append(send(c2, c2o.at[d], other))
        phase_top.append(send(z2, z2o.at[d], other))
    points_rest.wait_recv()
    points_three.append(send(p2.at[rest, :], p3.at[rest, :], flip(1)))

    side = mm(nvs[0, 0], couple(z1s[0], z1[...]))
    for i in (1, 2):
        side = side + mm(nvs[i, 0], couple(z1s[i], z1[...]))

    first = near[0, 0] - me
    second = near[0, 1] - me
    one = 1 - 2 * (me % 2)
    near_one = jnp.logical_or(first == one, second == one)

    def choose(a, b):
        return jnp.where(near_one, a.astype(F32), b.astype(F32)).astype(BF16)

    phase_rhs = []

    def relay(c):
        rhs_two[c].wait_recv()
        rows = pl.ds(c * step, step)
        phase_rhs.append(send(r2.at[rows, :], r3.at[rows, :], flip(1)))

    def near_chunk(c, final):
        rows = pl.ds(c * step, step)
        phase_rhs[c].wait_recv()
        picked = choose(p1[rows, :], p2[rows, :])
        cp[0:step, 0:dim] = picked
        cp[0:step, dim:] = norm_lanes(picked, 1.0, 1.0, True)
        diagonal = p3[rows, :]
        cp[step:, 0:dim] = diagonal
        cp[step:, dim:] = norm_lanes(diagonal, 1.0, 1.0, True)
        cr[0:step, :] = choose(r1[rows, :], r2[rows, :])
        cr[step:, :] = r3[rows, :]

        def body(block, carry):
            rows = pl.ds(pl.multiple_of(block * ROWS, ROWS), ROWS)
            value = acc[rows, :] + mm(tiles(rows, cp, 2 * step), cr[...])
            if final:
                out[rows, :] = value.astype(BF16)
            else:
                acc[rows, :] = value
            return carry

        lax.fori_loop(0, blocks, body, 0, unroll=2)

    relay(0)
    rhs_one.wait_recv()
    points_one.wait_recv()
    for copy in points_three:
        copy.wait_recv()
    relay(1)
    near_chunk(0, False)
    for copy in phase_top:
        copy.wait_recv()
    field = mm(c2o[0], couple(z2o[0], z2[...]))
    for d in range(1, nodes - 1):
        field = field + mm(c2o[d], couple(z2o[d], z2[...]))
    field1 = side + mm(field.astype(BF16), nl[...], 1, 1)
    f1[mine, :] = field1.astype(BF16)
    down_two = send(f1.at[mine, :], f1.at[mine, :], flip(2))
    phase_down = [send(f1.at[mine, :], f1.at[mine, :], flip(1))]
    for c in range(EARLY, CHUNKS):
        send_chunk(c)
    for c in range(2, CHUNKS):
        relay(c)
        near_chunk(c - 1, False)
        if c == CHUNKS - 2:
            down_two.wait_recv()
            phase_down.append(send(f1.at[at_slot(2), :], f1.at[at_slot(2), :], flip(1)))
        if c == CHUNKS - 1:
            for copy in phase_far:
                copy.wait_recv()
            for copy in phase_down:
                copy.wait_recv()
            far_z = choose(z0x[1], z0x[0])
            far_c = choose(c0x[1], c0x[0])
            field0 = mm(far_c, couple(far_z, z0[...])) + mm(f1[...], lift[...].astype(BF16), 1, 1)
            c0x[0] = field0.astype(BF16)

            def descend(block, carry):
                rows = pl.ds(pl.multiple_of(block * ROWS, ROWS), ROWS)
                acc[rows, :] += mm(bases[rows, :], c0x[0], 1, 1)
                return carry

            lax.fori_loop(0, blocks, descend, 0)
    near_chunk(CHUNKS - 1, True)
    for copy in started:
        copy.wait_send()


def per_device(n, near, points, charges, order, bases, lift, nlift, zleaf, znode, ztop):
    leaf, dim = points.shape
    nrhs = charges.shape[1]
    rank = lift.shape[0]
    quarter = rank // 4
    nodes = n // 16
    copies = 8 + 2 + 1 + 3 + 2 + CHUNKS + 4 + 6 + 3 + 2 + 2 * (nodes - 1) + CHUNKS + 3
    v = pltpu.VMEM
    vmem = pl.BlockSpec(memory_space=pltpu.VMEM)
    return pl.pallas_call(
        functools.partial(kernel, n),
        out_shape=jax.ShapeDtypeStruct((leaf, nrhs), BF16),
        in_specs=[pl.BlockSpec(memory_space=pltpu.SMEM)] + [pl.BlockSpec(memory_space=pl.ANY)] * 3 + [vmem] * 6,
        out_specs=vmem,
        scratch_shapes=[
            v((leaf, dim), BF16), v((leaf, nrhs), BF16), v((leaf, rank), BF16),
            v((leaf, nrhs), BF16), v((leaf, 2 * dim), BF16), v((leaf, 2 * dim), BF16),
            v((leaf, nrhs), F32),
            v((leaf, dim), BF16), v((leaf, dim), BF16), v((leaf, dim), BF16),
            v((leaf, nrhs), BF16), v((leaf, nrhs), BF16), v((leaf, nrhs), BF16),
            v((2 * leaf // CHUNKS, 2 * dim), BF16), v((2 * leaf // CHUNKS, nrhs), BF16),
            v((nrhs, rank), BF16), v((2, nrhs, rank), BF16),
            v((rank, dim), BF16), v((2, rank, dim), BF16),
            v((nrhs, rank), BF16), v((quarter, rank), BF16), v((3, quarter, rank), BF16),
            v((rank, rank), BF16), v((rank, dim), BF16), v((3, rank, dim), BF16),
            v((rank, dim), BF16),
            v((2, quarter, rank), BF16), v((3, 2, quarter, rank), BF16),
            v((quarter, rank), BF16), v((nodes - 1, quarter, rank), BF16),
            v((nodes - 1, rank, dim), BF16), v((nrhs, rank), BF16),
            pltpu.SemaphoreType.DMA((copies,)), pltpu.SemaphoreType.DMA((copies,)),
            pltpu.SemaphoreType.DMA((3,)),
        ],
        compiler_params=pltpu.CompilerParams(
            collective_id=0, has_side_effects=True, vmem_limit_bytes=60 * 1024 * 1024),
    )(near, points, charges, bases, order, lift, nlift, zleaf, znode, ztop)


def solution(mesh):
    n = mesh.shape["leaf"]

    def body(points, charges, order, near, bases, lift, nlift, zleaf, znode, ztop):
        return per_device(n, near, points, charges, order, bases, lift, nlift, zleaf, znode, ztop)

    return jax.shard_map(
        body, mesh=mesh, in_specs=(P("leaf", None),) * 10, out_specs=P("leaf", None), check_vma=False)
```

profile of v0, /device:TPU:0, one launch (start us, length us, event | category | flops | bytes accessed | tf_op | source)
XLA Modules:
  0.0 56.0 jit_solution(12562611784121899455)
XLA Ops:
  0.0 53.7 %shard_map.100 = bf16[2048,256]{1,0:T(8,128)(2,1)} custom-call(s32[1,2]{1,0:T(1,128)} %near.1, bf16[2048,128]{1,0:T(8,128)(2,1)} %points_in.1, bf16[2048,256]{1,0:T(8,128)(2,1)} %charges_in.1, bf16[2048,256]{1,0:T(8,128)(2,1)} %bases_in.1, s32[1,2048]{1,0:T(1,128)} %order.1, f32[256,256]{1,0:T(8,128)} %lift.1, f32[64,256]{1,0:T(8,128)} %nlift.1, ...), custom_call_target="tpu_custom_call" | custom-call | tf_op jit(solution)/shard_map/pallas_call | solution.py:337
  53.7 2.3 %copy.12 = bf16[2048,256]{1,0:T(8,128)(2,1)} copy(bf16[2048,256]{1,0:T(8,128)(2,1)} %shard_map.100) | data formatting | bytes 2097152
where the time goes:
time: 56.1 us; the launch traced here: 56 us
  Pallas kernels  53.7 us (96%)
  local copies, waits for them, and re-layouts  2.26 us (4%)
    pallas_call x1, Pallas kernels, per_device(): pl.pallas_call(functools.partial(kernel, n), out_shape=jax.ShapeDtypeStru...  53.7 us
    unnamed x1, local copies, waits for them, and re-layouts  2.26 us

commit v1 on v0

v1 whole, which is shorter than its diff:
```python
import functools

import jax
import jax.numpy as jnp
from jax import lax
from jax.experimental import pallas as pl
from jax.experimental.pallas import tpu as pltpu
from jax.sharding import PartitionSpec as P

MESH = pl.DeviceIdType.MESH
F32, BF16 = jnp.float32, jnp.bfloat16
CHUNKS = 8
PARTS = 4
ROWS = 1024
VMEM_MB = 50


def mm(a, b, ca=1, cb=0):
    return lax.dot_general(a, b, (((ca,), (cb,)), ((), ())), preferred_element_type=F32)


def split3(x):
    high = x.astype(BF16).astype(F32)
    middle = (x - high).astype(BF16).astype(F32)
    return high, middle, x - high - middle


def norm_column(p):
    wide = p.astype(F32)
    return jnp.sum(wide * wide, axis=1, keepdims=True)


def norm_lanes(p, one_scale, norm_scale, norm_first):
    high, middle, low = split3(norm_column(p))
    lane = lax.broadcasted_iota(jnp.int32, (p.shape[0], 128), 1)
    first = 0 if norm_first else 3
    ones = jnp.where(lane < 6, one_scale, 0.0)
    out = jnp.where(lane == first, high * norm_scale, ones)
    out = jnp.where(lane == first + 1, middle * norm_scale, out)
    out = jnp.where(lane == first + 2, low * norm_scale, out)
    return out.astype(BF16)


def couple(left, right):
    scale = 2.0 / left.shape[1]
    wide = right.astype(F32)
    square = wide * wide
    high = square.astype(BF16)
    low = (square - high.astype(F32)).astype(BF16)
    ones = jnp.ones((8, left.shape[1]), BF16)
    right_norm = (mm(ones, high, 1, 1) + mm(ones, low, 1, 1))[0:1, :]
    return jnp.exp((2.0 * mm(left, right, 1, 1) - norm_column(left) - right_norm) * scale).astype(BF16)


def kernel(n, near, points_in, charges_in, bases_in, order, lift, nlift, zleaf, znode, ztop, out,
           points, charges, bases, rhs, rhst, laug, raug, acc, p1, p2, p3, r1, r2, r3, rmask, prel,
           t1, t2, saug, cr, racc, dsend, drecv, xsend, xrecv, fsend, frecv,
           c0, c0x, z0, z0x, ut, us, rs, nl, z1, z1s, z2, nv, nvs, c2, c2o, z2o, f1, f0,
           ssem, rsem, lsem):
    me = lax.axis_index("leaf")
    leaf, dim = points.shape
    rank = lift.shape[0]
    quarter = rank // 4
    sixteenth = rank // 16
    nodes = n // 16
    slot = me % 4
    group = me // 4 % 4
    part = me % 16
    node = me // 16
    step = leaf // CHUNKS
    wide = leaf // PARTS
    half = PARTS // 2
    blocks = leaf // ROWS
    gives = (me // 2 + me // 4) % 2 == 0
    works = (me // 2 + me // 4) % 2 == 1

    def flip(bits):
        where = me
        for bit in (1, 2, 4, 8):
            if bits & bit:
                where = where + bit - 2 * bit * (me // bit % 2)
        return where

    def flip_slot(bits):
        return flip(bits) % 4

    others = [(node + d) % nodes * 16 + part for d in range(1, nodes)]

    barrier = pltpu.get_barrier_semaphore()
    partners = [flip(b) for b in (1, 2, 4, 6, 8, 12)] + others
    for other in partners:
        pl.semaphore_signal(barrier, inc=1, device_id=(other,), device_id_type=MESH)

    loads = [pltpu.make_async_copy(a, b, lsem.at[i]) for i, (a, b) in enumerate(
        ((charges_in, charges), (bases_in, bases), (points_in, points)))]
    for copy in loads:
        copy.start()
    count = [0]

    def link(src, dst, device):
        i = count[0]
        count[0] += 1
        return pltpu.make_async_remote_copy(
            src_ref=src, dst_ref=dst, send_sem=ssem.at[i], recv_sem=rsem.at[i],
            device_id=(device,), device_id_type=MESH)

    started = []

    def send(src, dst, device):
        copy = link(src, dst, device)
        copy.start()
        started.append(copy)
        return copy

    def at_slot(bits):
        where = flip_slot(bits) if bits else slot
        return pl.ds(pl.multiple_of(where * quarter, quarter), quarter)

    mine = at_slot(0)
    mine16 = pl.ds(pl.multiple_of(part * sixteenth, sixteenth), sixteenth)
    far16 = pl.ds(pl.multiple_of(flip(2) % 16 * sixteenth, sixteenth), sixteenth)
    mine64 = pl.ds(pl.multiple_of(group * quarter, quarter), quarter)
    part_rows = [pl.ds(k * wide, wide) for k in range(PARTS)]
    step_rows = [pl.ds(j * step, step) for j in range(CHUNKS)]

    give_points = [link(points_in.at[r, :], p2.at[r, :], flip(2)) for r in part_rows[:half]]
    give_detour = [link(points_in.at[r, :], prel.at[pl.ds(k * wide, wide), :], flip(4))
                   for k, r in enumerate(part_rows[half:])]
    detour_on = [link(prel.at[pl.ds(k * wide, wide), :], p2.at[r, :], flip(6))
                 for k, r in enumerate(part_rows[half:])]
    give_proxy = link(z0, z0x.at[1], flip(2))
    give_coeff = link(c0, c0x.at[1], flip(2))
    give_rhs = [link(rhs.at[r, :], r2.at[r, :], flip(2)) for r in step_rows]
    share_points = [link(p2.at[r, :], p3.at[r, :], flip(1)) for r in part_rows]
    share_rhs = [link(r2.at[r, :], r3.at[r, :], flip(1)) for r in step_rows]
    cross_part = [link(dsend.at[k], drecv.at[k], flip(1)) for k in range(PARTS)]
    back_part = [link(xsend.at[k], xrecv.at[k], flip(2)) for k in range(PARTS)]
    back_far = link(fsend, frecv, flip(2))
    mate_rhs = link(rhs, r1, flip(1))
    up_two = link(us, rs.at[2], flip(2))
    phase_b = []
    for i, b in enumerate((4, 8, 12)):
        phase_b.append(link(z1, z1s.at[i], flip(b)))
        phase_b.append(link(z2.at[mine64, :], z2.at[mine64, :], flip(b)))
    phase_two = [link(nv, nvs.at[i], flip(b)) for i, b in enumerate((4, 8, 12))]
    phase_top = []
    for d, other in enumerate(others):
        phase_top.append(link(c2, c2o.at[d], other))
        phase_top.append(link(z2, z2o.at[d], other))
    down_two = link(f1.at[mine, :], f1.at[mine, :], flip(2))
    down_one = link(f1.at[mine, :], f1.at[mine, :], flip(1))
    down_rest = link(f1.at[at_slot(2), :], f1.at[at_slot(2), :], flip(1))

    z1[mine, :] = znode[...].astype(BF16)
    nl[mine, :] = nlift[...].astype(BF16)
    z2[mine16, :] = ztop[...].astype(BF16)
    z0[...] = zleaf[...].astype(BF16)
    pl.semaphore_wait(barrier, len(partners))

    phase_a2 = [send(z1.at[mine, :], z1.at[mine, :], flip(2)),
                send(nl.at[mine, :], nl.at[mine, :], flip(2)),
                send(z2.at[mine16, :], z2.at[mine16, :], flip(2))]

    @pl.when(gives)
    def _():
        for copy in give_points + give_detour + [give_proxy]:
            copy.start()

    phase_a = [send(z1.at[mine, :], z1.at[mine, :], flip(1)),
               send(nl.at[mine, :], nl.at[mine, :], flip(1)),
               send(z2.at[mine16, :], z2.at[mine16, :], flip(1))]
    mate_points = send(points_in, p1, flip(1))
    loads[0].wait()

    def permute(block, carry):
        rows = pl.ds(pl.multiple_of(block * wide, wide), wide)
        index = jnp.broadcast_to(order[0:1, rows].astype(F32), (128, wide)).T
        lane = lax.broadcasted_iota(jnp.int32, (wide, 128), 1).astype(F32)
        chosen = jnp.concatenate(
            [jnp.where(index == lane + 128.0 * j, 1.0, 0.0).astype(BF16) for j in range(leaf // 128)], 1)
        value = mm(chosen, charges[...])
        rhs[rows, :] = value.astype(BF16)
        rhst[:, rows] = value.T.astype(BF16)
        return carry

    lax.fori_loop(0, PARTS, permute, 0)

    loads[1].wait()
    own = mm(rhst[...], bases[...]).astype(BF16)
    c0[...] = own
    ut[...] = mm(own, lift[...].astype(BF16)).astype(BF16)
    up_near = send(ut.at[at_slot(1), :], rs.at[0], flip(1))
    up_cross = send(ut.at[at_slot(3), :], rs.at[1], flip(1))

    @pl.when(gives)
    def _():
        give_rhs[0].start()
        mate_rhs.start()

    mate_far = [send(c0, c0x.at[0], flip(1)), send(z0, z0x.at[0], flip(1))]
    for copy in phase_a2:
        copy.wait_recv()
    phase_a.append(send(z1.at[at_slot(2), :], z1.at[at_slot(2), :], flip(1)))
    phase_a.append(send(nl.at[at_slot(2), :], nl.at[at_slot(2), :], flip(1)))
    phase_a.append(send(z2.at[far16, :], z2.at[far16, :], flip(1)))
    loads[2].wait()

    def augment(block, carry):
        rows = pl.ds(pl.multiple_of(block * ROWS, ROWS), ROWS)
        p = points[rows, :]
        laug[rows, 0:dim] = (p.astype(F32) * (4.0 / dim)).astype(BF16)
        laug[rows, dim:] = norm_lanes(p, -2.0 / dim, -2.0 / dim, False)
        raug[rows, 0:dim] = p
        raug[rows, dim:] = norm_lanes(p, 1.0, 1.0, True)
        return carry

    first = near[0, 0] - me
    second = near[0, 1] - me
    one = 1 - 2 * (me % 2)
    near_one = jnp.logical_or(first == one, second == one)

    def choose(a, b):
        return jnp.where(near_one, a.astype(F32), b.astype(F32)).astype(BF16)

    def tiles(rows):
        left = laug[rows, :]
        return jnp.concatenate(
            [jnp.exp(mm(left, raug[j:j + 512, :], 1, 1)).astype(BF16) for j in range(0, leaf, 512)], 1)

    def own_tile(block):
        def body(b, carry):
            rows = pl.ds(pl.multiple_of(b * ROWS, ROWS), ROWS)
            acc[rows, :] = mm(tiles(rows), rhs[...])
            return carry

        lax.fori_loop(block, block + 1, body, 0)

    def carry_up():
        up_cross.wait_recv()
        us[...] = (ut[at_slot(2), :].astype(F32) + rs[1].astype(F32)).astype(BF16)
        up_two.start()

    def spread_proxies():
        for copy in phase_a:
            copy.wait_recv()
        for copy in phase_b:
            copy.start()

    def node_level():
        up_near.wait_recv()
        up_two.wait_recv()
        total = ut[mine, :].astype(F32) + rs[0].astype(F32) + rs[2].astype(F32)
        nv[0] = total.astype(BF16)
        nv[1] = mm(total.astype(BF16), nl[...]).astype(BF16)
        for copy in phase_two:
            copy.start()

    def top_level():
        for copy in phase_b + phase_two:
            copy.wait_recv()
        lifted = nv[1].astype(F32)
        for i in range(3):
            lifted = lifted + nvs[i, 1].astype(F32)
        c2[...] = lifted.astype(BF16)
        for copy in phase_top:
            copy.start()

    def fields_down():
        side = mm(nvs[0, 0], couple(z1s[0], z1[...]))
        for i in (1, 2):
            side = side + mm(nvs[i, 0], couple(z1s[i], z1[...]))
        for copy in phase_top:
            copy.wait_recv()
        field = mm(c2o[0], couple(z2o[0], z2[...]))
        for d in range(1, nodes - 1):
            field = field + mm(c2o[d], couple(z2o[d], z2[...]))
        field1 = side + mm(field.astype(BF16), nl[...], 1, 1)
        f1[mine, :] = field1.astype(BF16)
        down_two.start()
        down_one.start()

    def gather_down():
        down_two.wait_recv()
        down_rest.start()

    def descend(far):
        down_one.wait_recv()
        down_rest.wait_recv()
        f0[...] = (far() + mm(f1[...], lift[...].astype(BF16), 1, 1)).astype(BF16)

        def body(block, carry):
            rows = pl.ds(pl.multiple_of(block * ROWS, ROWS), ROWS)
            acc[rows, :] += mm(bases[rows, :], f0[...], 1, 1)
            return carry

        lax.fori_loop(0, blocks, body, 0)

    carry_up()
    lax.fori_loop(0, blocks, augment, 0)

    @pl.when(gives)
    def _():
        give_rhs[1].start()
        give_rhs[2].start()
        own_tile(0)
        spread_proxies()
        give_rhs[3].start()
        own_tile(1)
        node_level()
        give_rhs[4].start()
        mate_points.wait_recv()
        mate_rhs.wait_recv()

        def mate(block, carry):
            rows = pl.ds(pl.multiple_of(block * ROWS, ROWS), ROWS)
            p = p1[rows, :]
            raug[rows, 0:dim] = p
            raug[rows, dim:] = norm_lanes(p, 1.0, 1.0, True)
            rmask[rows, :] = jnp.where(near_one, r1[rows, :].astype(F32), 0.0).astype(BF16)
            return carry

        lax.fori_loop(0, blocks, mate, 0)

        def mate_tile(block):
            def body(b, carry):
                rows = pl.ds(pl.multiple_of(b * ROWS, ROWS), ROWS)
                acc[rows, :] += mm(tiles(rows), rmask[...])
                return carry

            lax.fori_loop(block, block + 1, body, 0)

        mate_tile(0)
        give_rhs[5].start()
        give_coeff.start()
        mate_tile(1)
        top_level()
        fields_down()
        give_rhs[6].start()
        give_rhs[7].start()
        gather_down()
        for copy in mate_far:
            copy.wait_recv()
        back_far.wait_recv()
        descend(lambda: jnp.where(
            near_one, frecv[...].astype(F32), mm(c0x[0], couple(z0x[0], z0[...]))))
        for k, copy in enumerate(back_part):
            copy.wait_recv()
            out[part_rows[k], :] = (acc[part_rows[k], :] + xrecv[k].astype(F32)).astype(BF16)
        for copy in (give_points + give_detour + [give_proxy, give_coeff] + give_rhs):
            copy.wait_send()

    @pl.when(works)
    def _():
        def take_points(k):
            (give_points[k] if k < half else detour_on[k - half]).wait_recv()
            share_points[k].start()

        def pass_on(k):
            give_detour[k].wait_recv()
            detour_on[k].start()

        def part(tile, k, picked):
            saug[:, 0:dim] = picked
            saug[:, dim:] = norm_lanes(picked, 1.0, 1.0, True)

            def body(block, carry):
                rows = pl.ds(pl.multiple_of(block * ROWS, ROWS), ROWS)
                tile[k, rows, :] = jnp.exp(mm(laug[rows, :], saug[...], 1, 1)).astype(BF16)
                return carry

            lax.fori_loop(0, blocks, body, 0)
            return mm(rhst[...], tile[k]).T

        def diagonal(k):
            share_points[k].wait_recv()
            dsend[k] = part(t2, k, p3[part_rows[k], :]).astype(BF16)
            cross_part[k].start()

        def chosen(k):
            value = part(t1, k, choose(p1[part_rows[k], :], p2[part_rows[k], :]))
            racc[...] = jnp.where(near_one, 0.0, value)

        def combine(k):
            cross_part[k].wait_recv()
            xsend[k] = (racc[...] + drecv[k].astype(F32)).astype(BF16)

        take_points(0)
        pass_on(0)
        diagonal(0)
        pass_on(1)
        mate_points.wait_recv()
        chosen(0)
        take_points(1)
        combine(0)
        back_part[0].start()
        diagonal(1)
        spread_proxies()
        chosen(1)
        take_points(2)
        combine(1)
        back_part[1].start()
        mate_rhs.start()
        diagonal(2)
        chosen(2)
        take_points(3)
        combine(2)
        back_part[2].start()
        node_level()
        diagonal(3)
        chosen(3)
        combine(3)
        give_proxy.wait_recv()
        fsend[...] = jnp.where(near_one, mm(c0[...], couple(z0[...], z0x[1])), 0.0).astype(BF16)
        top_level()
        own_tile(0)
        fields_down()
        back_far.start()
        back_part[3].start()

        def take_rhs(j):
            give_rhs[j].wait_recv()
            share_rhs[j].start()

        def apply(j, final):
            k, at = divmod(j * step, wide)
            cr[...] = choose(r1[step_rows[j], :], r2[step_rows[j], :])

            def body(block, carry):
                rows = pl.ds(pl.multiple_of(block * ROWS, ROWS), ROWS)
                value = acc[rows, :] + mm(t1[k, rows, at:at + step], cr[...])
                value = value + mm(t2[k, rows, at:at + step], r3[step_rows[j], :])
                if final:
                    out[rows, :] = value.astype(BF16)
                else:
                    acc[rows, :] = value
                return carry

            lax.fori_loop(0, blocks, body, 0)

        take_rhs(0)
        take_rhs(1)
        take_rhs(2)
        own_tile(1)
        mate_rhs.wait_recv()
        for j in range(CHUNKS):
            if j + 3 < CHUNKS:
                take_rhs(j + 3)
            share_rhs[j].wait_recv()
            if j == CHUNKS - 1:
                gather_down()
                for copy in mate_far:
                    copy.wait_recv()
                give_coeff.wait_recv()
                descend(lambda: mm(choose(c0x[1], c0x[0]), couple(choose(z0x[1], z0x[0]), z0[...])))
            apply(j, j == CHUNKS - 1)
        for copy in (detour_on + share_points + share_rhs + cross_part + back_part + [back_far]):
            copy.wait_send()

    for copy in started + [mate_rhs, up_two, down_two, down_one, down_rest] + phase_b + phase_two + phase_top:
        copy.wait_send()


def per_device(n, near, points, charges, order, bases, lift, nlift, zleaf, znode, ztop):
    leaf, dim = points.shape
    nrhs = charges.shape[1]
    rank = lift.shape[0]
    quarter = rank // 4
    nodes = n // 16
    wide, step = leaf // PARTS, leaf // CHUNKS
    copies = 60 + 3 * PARTS + 2 * CHUNKS + 2 * nodes
    v = pltpu.VMEM
    vmem = pl.BlockSpec(memory_space=pltpu.VMEM)
    return pl.pallas_call(
        functools.partial(kernel, n),
        out_shape=jax.ShapeDtypeStruct((leaf, nrhs), BF16),
        in_specs=[pl.BlockSpec(memory_space=pltpu.SMEM)] + [pl.BlockSpec(memory_space=pl.ANY)] * 3 + [vmem] * 6,
        out_specs=vmem,
        scratch_shapes=[
            v((leaf, dim), BF16), v((leaf, nrhs), BF16), v((leaf, rank), BF16),
            v((leaf, nrhs), BF16), v((nrhs, leaf), BF16), v((leaf, 2 * dim), BF16), v((leaf, 2 * dim), BF16),
            v((leaf, nrhs), F32),
            v((leaf, dim), BF16), v((leaf, dim), BF16), v((leaf, dim), BF16),
            v((leaf, nrhs), BF16), v((leaf, nrhs), BF16), v((leaf, nrhs), BF16), v((leaf, nrhs), BF16),
            v((leaf // 2, dim), BF16),
            v((PARTS, leaf, wide), BF16), v((PARTS, leaf, wide), BF16),
            v((wide, 2 * dim), BF16), v((step, nrhs), BF16), v((wide, nrhs), F32),
            v((PARTS, wide, nrhs), BF16), v((PARTS, wide, nrhs), BF16),
            v((PARTS, wide, nrhs), BF16), v((PARTS, wide, nrhs), BF16),
            v((nrhs, rank), BF16), v((nrhs, rank), BF16),
            v((nrhs, rank), BF16), v((2, nrhs, rank), BF16),
            v((rank, dim), BF16), v((2, rank, dim), BF16),
            v((nrhs, rank), BF16), v((quarter, rank), BF16), v((3, quarter, rank), BF16),
            v((rank, rank), BF16), v((rank, dim), BF16), v((3, rank, dim), BF16),
            v((rank, dim), BF16),
            v((2, quarter, rank), BF16), v((3, 2, quarter, rank), BF16),
            v((quarter, rank), BF16), v((nodes - 1, quarter, rank), BF16),
            v((nodes - 1, rank, dim), BF16), v((nrhs, rank), BF16), v((nrhs, rank), BF16),
            pltpu.SemaphoreType.DMA((copies,)), pltpu.SemaphoreType.DMA((copies,)),
            pltpu.SemaphoreType.DMA((3,)),
        ],
        compiler_params=pltpu.CompilerParams(
            collective_id=0, has_side_effects=True, vmem_limit_bytes=VMEM_MB * 1024 * 1024),
    )(near, points, charges, bases, order, lift, nlift, zleaf, znode, ztop)


def solution(mesh):
    n = mesh.shape["leaf"]

    def body(points, charges, order, near, bases, lift, nlift, zleaf, znode, ztop):
        return per_device(n, near, points, charges, order, bases, lift, nlift, zleaf, znode, ztop)

    return jax.shard_map(
        body, mesh=mesh, in_specs=(P("leaf", None),) * 10, out_specs=P("leaf", None), check_vma=False)
```

time: 56.1 us -> 63.1 us (1.12)
  the two profiles are of different devices: /device:TPU:0 before, /device:TPU:5 now
where the time goes in v1:
time: 63.1 us; the launch traced here: 62.7 us
  Pallas kernels  53.9 us (85%)
  local copies, waits for them, and re-layouts  8.73 us (14%)
    pallas_call x1, Pallas kernels, per_device(): pl.pallas_call(functools.partial(kernel, n), out_shape=jax.ShapeDtypeStru...  53.9 us
    unnamed x19, local copies, waits for them, and re-layouts  8.73 us

profile of v1, /device:TPU:5, one launch (start us, length us, event | category | flops | bytes accessed | tf_op | source)
XLA Modules:
  0.0 62.7 jit_solution(9036049545437664474)
XLA Ops:
  0.0 0.0 copy-start
  0.0 1.2 %copy-done = bf16[2048,256]{1,0:T(8,128)(2,1)S(1)} copy-done((bf16[2048,256]{1,0:T(8,128)(2,1)S(1)}, bf16[2048,256]{1,0:T(8,128)(2,1)}, u32[]{:S(2)}) %copy-start) | copy-done | bytes 1048600
  1.2 0.0 copy-start.1
  1.2 1.0 %copy-done.1 = bf16[2048,128]{1,0:T(8,128)(2,1)S(1)} copy-done((bf16[2048,128]{1,0:T(8,128)(2,1)S(1)}, bf16[2048,128]{1,0:T(8,128)(2,1)}, u32[]{:S(2)}) %copy-start.1) | copy-done | bytes 524312
  2.3 0.0 copy-start.2
  2.3 0.9 %copy-done.2 = f32[256,256]{1,0:T(8,128)S(1)} copy-done((f32[256,256]{1,0:T(8,128)S(1)}, f32[256,256]{1,0:T(8,128)}, u32[]{:S(2)}) %copy-start.2) | copy-done | bytes 262168
  3.2 0.0 copy-start.3
  3.2 0.9 %copy-done.3 = f32[256,128]{1,0:T(8,128)S(1)} copy-done((f32[256,128]{1,0:T(8,128)S(1)}, f32[256,128]{1,0:T(8,128)}, u32[]{:S(2)}) %copy-start.3) | copy-done | bytes 131096
  4.1 0.0 copy-start.4
  4.1 0.8 %copy-done.4 = f32[64,256]{1,0:T(8,128)S(1)} copy-done((f32[64,256]{1,0:T(8,128)S(1)}, f32[64,256]{1,0:T(8,128)}, u32[]{:S(2)}) %copy-start.4) | copy-done | bytes 65560
  5.0 0.0 copy-start.5
  5.0 0.8 %copy-done.5 = f32[64,128]{1,0:T(8,128)S(1)} copy-done((f32[64,128]{1,0:T(8,128)S(1)}, f32[64,128]{1,0:T(8,128)}, u32[]{:S(2)}) %copy-start.5) | copy-done | bytes 32792
  5.7 0.0 copy-start.6
  5.7 0.7 %copy-done.6 = s32[1,2048]{1,0:T(1,128)S(1)} copy-done((s32[1,2048]{1,0:T(1,128)S(1)}, s32[1,2048]{1,0:T(1,128)}, u32[]{:S(2)}) %copy-start.6) | copy-done | bytes 8216
  6.4 0.0 copy-start.7
  6.4 0.7 %copy-done.7 = f32[16,128]{1,0:T(8,128)S(1)} copy-done((f32[16,128]{1,0:T(8,128)S(1)}, f32[16,128]{1,0:T(8,128)}, u32[]{:S(2)}) %copy-start.7) | copy-done | bytes 8216
  7.1 0.0 copy-start.8
  7.1 0.7 %copy-done.8 = s32[1,2]{1,0:T(1,128)S(1)} copy-done((s32[1,2]{1,0:T(1,128)S(1)}, s32[1,2]{1,0:T(1,128)}, u32[]{:S(2)}) %copy-start.8) | copy-done | bytes 32
  7.8 53.9 %shard_map.100 = bf16[2048,256]{1,0:T(8,128)(2,1)S(1)} custom-call(s32[1,2]{1,0:T(1,128)S(1)} %copy-done.8, bf16[2048,128]{1,0:T(8,128)(2,1)S(1)} %copy-done.1, bf16[2048,256]{1,0:T(8,128)(2,1)S(1)} %copy-done, bf16[2048,256]{1,0:T(8,128)(2,1)} %bases_in.1, s32[1,2048]{1,0:T(1,128)S(1)} %copy-done.6, f32[256,256]{1,0:T(8,128)S(1)} %copy-done.2, ...), custom_call_target="tpu_custom_call" | custom-call | tf_op jit(solution)/shard_map/pallas_call | solution.py:473
  61.7 1.0 %copy.12 = bf16[2048,256]{1,0:T(8,128)(2,1)} copy(bf16[2048,256]{1,0:T(8,128)(2,1)S(1)} %shard_map.100) | data formatting | bytes 2097152
Async XLA Ops:
  0.0 1.2 %copy-start = (bf16[2048,256]{1,0:T(8,128)(2,1)S(1)}, bf16[2048,256]{1,0:T(8,128)(2,1)}, u32[]{:S(2)}) copy-start(bf16[2048,256]{1,0:T(8,128)(2,1)} %charges_in.1) | copy-start | bytes 3145732
  1.2 1.0 %copy-start.1 = (bf16[2048,128]{1,0:T(8,128)(2,1)S(1)}, bf16[2048,128]{1,0:T(8,128)(2,1)}, u32[]{:S(2)}) copy-start(bf16[2048,128]{1,0:T(8,128)(2,1)} %points_in.1) | copy-start | bytes 1572868
  2.3 0.9 %copy-start.2 = (f32[256,256]{1,0:T(8,128)S(1)}, f32[256,256]{1,0:T(8,128)}, u32[]{:S(2)}) copy-start(f32[256,256]{1,0:T(8,128)} %lift.1) | copy-start | bytes 786436
  3.2 0.9 %copy-start.3 = (f32[256,128]{1,0:T(8,128)S(1)}, f32[256,128]{1,0:T(8,128)}, u32[]{:S(2)}) copy-start(f32[256,128]{1,0:T(8,128)} %zleaf.1) | copy-start | bytes 393220
  4.1 0.8 %copy-start.4 = (f32[64,256]{1,0:T(8,128)S(1)}, f32[64,256]{1,0:T(8,128)}, u32[]{:S(2)}) copy-start(f32[64,256]{1,0:T(8,128)} %nlift.1) | copy-start | bytes 196612
  5.0 0.8 %copy-start.5 = (f32[64,128]{1,0:T(8,128)S(1)}, f32[64,128]{1,0:T(8,128)}, u32[]{:S(2)}) copy-start(f32[64,128]{1,0:T(8,128)} %znode.1) | copy-start | bytes 98308
  5.7 0.7 %copy-start.6 = (s32[1,2048]{1,0:T(1,128)S(1)}, s32[1,2048]{1,0:T(1,128)}, u32[]{:S(2)}) copy-start(s32[1,2048]{1,0:T(1,128)} %order.1) | copy-start | bytes 24580
  6.4 0.7 %copy-start.7 = (f32[16,128]{1,0:T(8,128)S(1)}, f32[16,128]{1,0:T(8,128)}, u32[]{:S(2)}) copy-start(f32[16,128]{1,0:T(8,128)} %ztop.1) | copy-start | bytes 24580
  7.1 0.7 %copy-start.8 = (s32[1,2]{1,0:T(1,128)S(1)}, s32[1,2]{1,0:T(1,128)}, u32[]{:S(2)}) copy-start(s32[1,2]{1,0:T(1,128)} %near.1) | copy-start | bytes 28

commit v2 on v1

v2 whole, which is shorter than its diff:
```python
import functools

import jax
import jax.numpy as jnp
from jax import lax
from jax.experimental import pallas as pl
from jax.experimental.pallas import tpu as pltpu
from jax.sharding import PartitionSpec as P

MESH = pl.DeviceIdType.MESH
F32, BF16 = jnp.float32, jnp.bfloat16
CHUNKS = 8
PARTS = 4
ROWS = 1024
VMEM_MB = 50


def mm(a, b, ca=1, cb=0):
    return lax.dot_general(a, b, (((ca,), (cb,)), ((), ())), preferred_element_type=F32)


def split3(x):
    high = x.astype(BF16).astype(F32)
    middle = (x - high).astype(BF16).astype(F32)
    return high, middle, x - high - middle


def norm_column(p):
    wide = p.astype(F32)
    return jnp.sum(wide * wide, axis=1, keepdims=True)


def norm_lanes(p, one_scale, norm_scale, norm_first):
    high, middle, low = split3(norm_column(p))
    lane = lax.broadcasted_iota(jnp.int32, (p.shape[0], 128), 1)
    first = 0 if norm_first else 3
    ones = jnp.where(lane < 6, one_scale, 0.0)
    out = jnp.where(lane == first, high * norm_scale, ones)
    out = jnp.where(lane == first + 1, middle * norm_scale, out)
    out = jnp.where(lane == first + 2, low * norm_scale, out)
    return out.astype(BF16)


def couple(left, right):
    scale = 2.0 / left.shape[1]
    wide = right.astype(F32)
    square = wide * wide
    high = square.astype(BF16)
    low = (square - high.astype(F32)).astype(BF16)
    ones = jnp.ones((8, left.shape[1]), BF16)
    right_norm = (mm(ones, high, 1, 1) + mm(ones, low, 1, 1))[0:1, :]
    return jnp.exp((2.0 * mm(left, right, 1, 1) - norm_column(left) - right_norm) * scale).astype(BF16)


def kernel(n, near_in, points_in, charges_in, bases_in, order_in, lift_in, nlift_in, zleaf_in, znode_in, ztop_in, out,
           near, points, charges, bases, order, lift, nlift, zleaf, znode, ztop, rhs, laug, raug, acc, acct,
           p1, p2, p3, r1, r2, r3, rmask, prel,
           t1, t2, saug, racc, dsend, drecv, xsend, xrecv, fsend, frecv,
           c0, c0x, z0, z0x, ut, us, rs, nl, z1, z1s, z2, nv, nvs, c2, c2o, z2o, f1, f0,
           ssem, rsem, lsem):
    me = lax.axis_index("leaf")
    leaf, dim = points.shape
    rank = lift.shape[0]
    quarter = rank // 4
    sixteenth = rank // 16
    nodes = n // 16
    slot = me % 4
    group = me // 4 % 4
    part = me % 16
    node = me // 16
    step = leaf // CHUNKS
    wide = leaf // PARTS
    half = PARTS // 2
    blocks = leaf // ROWS
    gives = (me // 2 + me // 4) % 2 == 0
    works = (me // 2 + me // 4) % 2 == 1

    def flip(bits):
        where = me
        for bit in (1, 2, 4, 8):
            if bits & bit:
                where = where + bit - 2 * bit * (me // bit % 2)
        return where

    def flip_slot(bits):
        return flip(bits) % 4

    others = [(node + d) % nodes * 16 + part for d in range(1, nodes)]

    barrier = pltpu.get_barrier_semaphore()
    partners = [flip(b) for b in (1, 2, 4, 6, 8, 12)] + others
    for other in partners:
        pl.semaphore_signal(barrier, inc=1, device_id=(other,), device_id_type=MESH)

    loads = [pltpu.make_async_copy(a, b, lsem.at[i]) for i, (a, b) in enumerate((
        (znode_in, znode), (nlift_in, nlift), (ztop_in, ztop), (zleaf_in, zleaf), (order_in, order), (charges_in, charges),
        (bases_in, bases), (lift_in, lift), (points_in, points), (near_in, near)))]
    for copy in loads:
        copy.start()
    def start(copies):
        for copy in copies:
            copy.start()

    def arrive(copies):
        for copy in copies:
            copy.wait_recv()

    count = [0]

    def link(src, dst, device):
        i = count[0]
        count[0] += 1
        return pltpu.make_async_remote_copy(
            src_ref=src, dst_ref=dst, send_sem=ssem.at[i], recv_sem=rsem.at[i],
            device_id=(device,), device_id_type=MESH)

    def at_slot(bits):
        where = flip_slot(bits) if bits else slot
        return pl.ds(pl.multiple_of(where * quarter, quarter), quarter)

    mine = at_slot(0)
    mine16 = pl.ds(pl.multiple_of(part * sixteenth, sixteenth), sixteenth)
    far16 = pl.ds(pl.multiple_of(flip(2) % 16 * sixteenth, sixteenth), sixteenth)
    mine64 = pl.ds(pl.multiple_of(group * quarter, quarter), quarter)
    part_rows = [pl.ds(k * wide, wide) for k in range(PARTS)]
    step_rows = [pl.ds(j * step, step) for j in range(CHUNKS)]

    give_points = [link(points_in.at[r, :], p2.at[r, :], flip(2)) for r in part_rows[:half]]
    give_detour = [link(points_in.at[r, :], prel.at[pl.ds(k * wide, wide), :], flip(4))
                   for k, r in enumerate(part_rows[half:])]
    detour_on = [link(prel.at[pl.ds(k * wide, wide), :], p2.at[r, :], flip(6))
                 for k, r in enumerate(part_rows[half:])]
    give_proxy = link(z0, z0x.at[1], flip(2))
    give_coeff = link(c0, c0x.at[1], flip(2))
    give_rhs = [link(rhs.at[r, :], r2.at[r, :], flip(2)) for r in step_rows]
    share_points = [link(p2.at[r, :], p3.at[r, :], flip(1)) for r in part_rows]
    share_rhs = [link(r2.at[r, :], r3.at[r, :], flip(1)) for r in step_rows]
    cross_part = [link(dsend.at[k], drecv.at[k], flip(1)) for k in range(PARTS)]
    back_part = [link(xsend.at[k], xrecv.at[k], flip(2)) for k in range(PARTS)]
    back_far = link(fsend, frecv, flip(2))
    proxies_two = [link(z1.at[mine, :], z1.at[mine, :], flip(2)),
                   link(nl.at[mine, :], nl.at[mine, :], flip(2)),
                   link(z2.at[mine16, :], z2.at[mine16, :], flip(2))]
    proxies_one = [link(z1.at[mine, :], z1.at[mine, :], flip(1)),
                   link(nl.at[mine, :], nl.at[mine, :], flip(1)),
                   link(z2.at[mine16, :], z2.at[mine16, :], flip(1))]
    proxies_rest = [link(z1.at[at_slot(2), :], z1.at[at_slot(2), :], flip(1)),
                    link(nl.at[at_slot(2), :], nl.at[at_slot(2), :], flip(1)),
                    link(z2.at[far16, :], z2.at[far16, :], flip(1))]
    mate_points = link(points_in, p1, flip(1))
    mate_far = [link(c0, c0x.at[0], flip(1)), link(z0, z0x.at[0], flip(1))]
    up_near = link(ut.at[at_slot(1), :], rs.at[0], flip(1))
    up_cross = link(ut.at[at_slot(3), :], rs.at[1], flip(1))
    mate_rhs = link(rhs, r1, flip(1))
    up_two = link(us, rs.at[2], flip(2))
    phase_b = []
    for i, b in enumerate((4, 8, 12)):
        phase_b.append(link(z1, z1s.at[i], flip(b)))
        phase_b.append(link(z2.at[mine64, :], z2.at[mine64, :], flip(b)))
    phase_two = [link(nv, nvs.at[i], flip(b)) for i, b in enumerate((4, 8, 12))]
    top_proxies = [link(z2, z2o.at[d], other) for d, other in enumerate(others)]
    top_coeffs = [link(c2, c2o.at[d], other) for d, other in enumerate(others)]
    down_two = link(f1.at[mine, :], f1.at[mine, :], flip(2))
    down_one = link(f1.at[mine, :], f1.at[mine, :], flip(1))
    down_rest = link(f1.at[at_slot(2), :], f1.at[at_slot(2), :], flip(1))

    for copy in loads[:4]:
        copy.wait()
    z1[mine, :] = znode[...].astype(BF16)
    nl[mine, :] = nlift[...].astype(BF16)
    z2[mine16, :] = ztop[...].astype(BF16)
    z0[...] = zleaf[...].astype(BF16)

    def enter(copies):
        pl.semaphore_wait(barrier, len(partners))
        start(copies)

    @pl.when(gives)
    def _():
        enter(give_points[:1] + proxies_two + give_points[1:] + give_detour + [give_proxy] + proxies_one + [mate_points])

    loads[4].wait()
    loads[5].wait()

    def permute(block, carry):
        rows = pl.ds(pl.multiple_of(block * wide, wide), wide)
        index = jnp.broadcast_to(order[0:1, rows].astype(F32), (128, wide)).T
        lane = lax.broadcasted_iota(jnp.int32, (wide, 128), 1).astype(F32)
        chosen = jnp.concatenate(
            [jnp.where(index == lane + 128.0 * j, 1.0, 0.0).astype(BF16) for j in range(leaf // 128)], 1)
        value = mm(chosen, charges[...])
        rhs[rows, :] = value.astype(BF16)
        return carry

    lax.fori_loop(0, PARTS, permute, 0)

    @pl.when(works)
    def _():
        enter(proxies_two + proxies_one + [mate_points])

    loads[6].wait()
    loads[7].wait()
    own = mm(rhs[...], bases[...], 0, 0).astype(BF16)
    c0[...] = own
    ut[...] = mm(own, lift[...].astype(BF16)).astype(BF16)
    start([up_near, up_cross] + mate_far)
    loads[8].wait()
    loads[9].wait()

    def augment(block, carry):
        rows = pl.ds(pl.multiple_of(block * ROWS, ROWS), ROWS)
        p = points[rows, :]
        laug[rows, 0:dim] = (p.astype(F32) * (4.0 / dim)).astype(BF16)
        laug[rows, dim:] = norm_lanes(p, -2.0 / dim, -2.0 / dim, False)
        raug[rows, 0:dim] = p
        raug[rows, dim:] = norm_lanes(p, 1.0, 1.0, True)
        return carry

    first = near[0, 0] - me
    second = near[0, 1] - me
    one = 1 - 2 * (me % 2)
    near_one = jnp.logical_or(first == one, second == one)

    def choose(a, b):
        return jnp.where(near_one, a.astype(F32), b.astype(F32)).astype(BF16)

    def tiles(rows):
        left = laug[rows, :]
        return jnp.concatenate(
            [jnp.exp(mm(left, raug[j:j + 512, :], 1, 1)).astype(BF16) for j in range(0, leaf, 512)], 1)

    def own_tile(first, last):
        def body(b, carry):
            rows = pl.ds(pl.multiple_of(b * ROWS, ROWS), ROWS)
            acc[rows, :] = mm(tiles(rows), rhs[...])
            return carry

        lax.fori_loop(first, last, body, 0)

    def carry_up():
        us[...] = (ut[at_slot(2), :].astype(F32) + rs[1].astype(F32)).astype(BF16)

    def node_level():
        total = ut[mine, :].astype(F32) + rs[0].astype(F32) + rs[2].astype(F32)
        nv[0] = total.astype(BF16)
        nv[1] = mm(total.astype(BF16), nl[...]).astype(BF16)

    def top_level():
        lifted = nv[1].astype(F32)
        for i in range(3):
            lifted = lifted + nvs[i, 1].astype(F32)
        c2[...] = lifted.astype(BF16)

    def fields_down():
        side = mm(nvs[0, 0], couple(z1s[0], z1[...]))
        for i in (1, 2):
            side = side + mm(nvs[i, 0], couple(z1s[i], z1[...]))
        field = mm(c2o[0], couple(z2o[0], z2[...]))
        for d in range(1, nodes - 1):
            field = field + mm(c2o[d], couple(z2o[d], z2[...]))
        field1 = side + mm(field.astype(BF16), nl[...], 1, 1)
        f1[mine, :] = field1.astype(BF16)

    def descend(far):
        f0[...] = (far() + mm(f1[...], lift[...].astype(BF16), 1, 1)).astype(BF16)

        def body(block, carry):
            rows = pl.ds(pl.multiple_of(block * ROWS, ROWS), ROWS)
            acc[rows, :] += mm(bases[rows, :], f0[...], 1, 1)
            return carry

        lax.fori_loop(0, blocks, body, 0)

    lax.fori_loop(0, blocks, augment, 0)

    @pl.when(gives)
    def _():
        arrive([up_cross])
        carry_up()
        start([up_two, give_rhs[0], mate_rhs])
        arrive(proxies_two)
        start(proxies_rest + [give_rhs[1]])
        own_tile(0, blocks // 2)
        arrive(proxies_one + proxies_rest + [up_near, up_two])
        start(phase_b)
        node_level()
        start(phase_two + give_rhs[2:4])
        own_tile(blocks // 2, blocks)
        arrive(phase_b + [mate_points, mate_rhs])
        start(top_proxies + [give_rhs[4]])

        def mate(block, carry):
            rows = pl.ds(pl.multiple_of(block * ROWS, ROWS), ROWS)
            p = p1[rows, :]
            raug[rows, 0:dim] = p
            raug[rows, dim:] = norm_lanes(p, 1.0, 1.0, True)
            rmask[rows, :] = jnp.where(near_one, r1[rows, :].astype(F32), 0.0).astype(BF16)
            return carry

        lax.fori_loop(0, blocks, mate, 0)

        def mate_tile(b, carry):
            rows = pl.ds(pl.multiple_of(b * ROWS, ROWS), ROWS)
            acc[rows, :] += mm(tiles(rows), rmask[...])
            return carry

        lax.fori_loop(0, blocks, mate_tile, 0)
        start([give_rhs[5], give_coeff])
        arrive(phase_two)
        top_level()
        start(top_coeffs)
        arrive(top_proxies + top_coeffs)
        fields_down()
        start([down_two, down_one] + give_rhs[6:])
        arrive([down_two])
        start([down_rest])
        arrive([down_one, down_rest, back_far] + mate_far)
        descend(lambda: jnp.where(
            near_one, frecv[...].astype(F32), mm(c0x[0], couple(z0x[0], z0[...]))))
        for k, copy in enumerate(back_part):
            copy.wait_recv()
            out[part_rows[k], :] = (acc[part_rows[k], :] + xrecv[k].astype(F32)).astype(BF16)
        for copy in give_points + give_detour + [give_proxy, give_coeff] + give_rhs:
            copy.wait_send()

    @pl.when(works)
    def _():
        def part(tile, k, picked):
            saug[k % 2, :, 0:dim] = picked
            saug[k % 2, :, dim:] = norm_lanes(picked, 1.0, 1.0, True)
            values = jnp.concatenate(
                [jnp.exp(mm(saug[k % 2], laug[j:j + 512, :], 1, 1)).astype(BF16) for j in range(0, leaf, 512)], 1)
            tile[part_rows[k], :] = values
            return mm(values, rhs[...])

        def diagonal(k):
            dsend[k] = part(t2, k, p3[part_rows[k], :]).astype(BF16)

        def chosen(k):
            value = part(t1, k, choose(p1[part_rows[k], :], p2[part_rows[k], :]))
            racc[k % 2] = jnp.where(near_one, 0.0, value)

        def combine(k):
            xsend[k] = (racc[k % 2] + drecv[k].astype(F32)).astype(BF16)

        arrive([give_points[0], mate_points, up_cross])
        start([share_points[0]])
        carry_up()
        start([up_two])
        arrive([give_detour[0]])
        start([detour_on[0]])
        chosen(0)
        arrive([share_points[0]] + proxies_two)
        start(proxies_rest)
        diagonal(0)
        start([cross_part[0]])
        arrive([give_points[1], give_detour[1]])
        start([share_points[1], detour_on[1]])
        chosen(1)
        arrive([cross_part[0]])
        combine(0)
        start([back_part[0]])
        arrive([share_points[1]] + proxies_one + proxies_rest)
        start(phase_b)
        diagonal(1)
        start([cross_part[1]])
        arrive([detour_on[0]])
        start([share_points[2]])
        chosen(2)
        arrive([cross_part[1], share_points[2], detour_on[1], up_near, up_two])
        start([share_points[3]])
        node_level()
        start(phase_two)
        combine(1)
        diagonal(2)
        start([back_part[1], cross_part[2]])
        arrive([share_points[3]] + phase_b)
        start(top_proxies)
        chosen(3)
        arrive([cross_part[2]])
        combine(2)
        diagonal(3)
        start([back_part[2], cross_part[3], mate_rhs])
        arrive(phase_two + [give_proxy])
        top_level()
        fsend[...] = jnp.where(near_one, mm(c0[...], couple(z0[...], z0x[1])), 0.0).astype(BF16)
        start(top_coeffs + [back_far])
        arrive(give_rhs[:3] + [cross_part[3]])
        start(share_rhs[:3])
        combine(3)
        own_tile(0, blocks)
        arrive(top_proxies + top_coeffs + give_rhs[3:5])
        start(share_rhs[3:5])
        fields_down()
        start([down_two, down_one, back_part[3]])

        def pick_rhs(rows):
            return choose(r1[rows, :], r2[rows, :]), r3[rows, :]

        def apply(first, last):
            rows = pl.ds(first * step, (last - first) * step)
            near_rhs, far_rhs = pick_rhs(rows)
            value = mm(near_rhs, t1[rows, :], 0, 0) + mm(far_rhs, t2[rows, :], 0, 0)
            acct[...] = value if first == 0 else acct[...] + value

        def finish(j):
            near_rhs, far_rhs = pick_rhs(step_rows[j])
            return mm(t1[step_rows[j], :], near_rhs, 0, 0) + mm(t2[step_rows[j], :], far_rhs, 0, 0)

        arrive(share_rhs[:4] + [mate_rhs])
        apply(0, 4)
        arrive([give_rhs[5], down_two])
        start([share_rhs[5], down_rest])
        arrive([down_one, give_coeff, share_rhs[4], share_rhs[5]] + mate_far)
        apply(4, 6)
        arrive([down_rest])
        descend(lambda: mm(choose(c0x[1], c0x[0]), couple(choose(z0x[1], z0x[0]), z0[...])))
        for j in range(PARTS):
            acc[part_rows[j], :] += acct[:, j * wide:(j + 1) * wide].T
        arrive([give_rhs[6]])
        start([share_rhs[6]])
        arrive([share_rhs[6]])
        acc[...] += finish(6)
        arrive([give_rhs[7]])
        start([share_rhs[7]])
        arrive([share_rhs[7]])
        out[...] = (acc[...] + finish(7)).astype(BF16)
        for copy in detour_on + share_points + share_rhs + cross_part + back_part + [back_far]:
            copy.wait_send()

    for copy in (proxies_two + proxies_one + proxies_rest + mate_far + phase_b + phase_two + top_proxies + top_coeffs
                 + [mate_points, mate_rhs, up_near, up_cross, up_two, down_two, down_one, down_rest]):
        copy.wait_send()


def per_device(n, near, points, charges, order, bases, lift, nlift, zleaf, znode, ztop):
    leaf, dim = points.shape
    nrhs = charges.shape[1]
    rank = lift.shape[0]
    quarter = rank // 4
    nodes = n // 16
    wide, step = leaf // PARTS, leaf // CHUNKS
    copies = 60 + 3 * PARTS + 2 * CHUNKS + 2 * nodes
    v = pltpu.VMEM
    vmem = pl.BlockSpec(memory_space=pltpu.VMEM)
    return pl.pallas_call(
        functools.partial(kernel, n),
        out_shape=jax.ShapeDtypeStruct((leaf, nrhs), BF16),
        in_specs=[pl.BlockSpec(memory_space=pltpu.HBM)] * 10,
        out_specs=vmem,
        scratch_shapes=[
            pltpu.SMEM(near.shape, near.dtype),
            v((leaf, dim), BF16), v((leaf, nrhs), BF16), v((leaf, rank), BF16), v(order.shape, order.dtype),
            v(lift.shape, F32), v(nlift.shape, F32), v(zleaf.shape, F32), v(znode.shape, F32), v(ztop.shape, F32),
            v((leaf, nrhs), BF16), v((leaf, 2 * dim), BF16), v((leaf, 2 * dim), BF16),
            v((leaf, nrhs), F32), v((nrhs, leaf), F32),
            v((leaf, dim), BF16), v((leaf, dim), BF16), v((leaf, dim), BF16),
            v((leaf, nrhs), BF16), v((leaf, nrhs), BF16), v((leaf, nrhs), BF16), v((leaf, nrhs), BF16),
            v((leaf // 2, dim), BF16),
            v((leaf, leaf), BF16), v((leaf, leaf), BF16),
            v((2, wide, 2 * dim), BF16), v((2, wide, nrhs), F32),
            v((PARTS, wide, nrhs), BF16), v((PARTS, wide, nrhs), BF16),
            v((PARTS, wide, nrhs), BF16), v((PARTS, wide, nrhs), BF16),
            v((nrhs, rank), BF16), v((nrhs, rank), BF16),
            v((nrhs, rank), BF16), v((2, nrhs, rank), BF16),
            v((rank, dim), BF16), v((2, rank, dim), BF16),
            v((nrhs, rank), BF16), v((quarter, rank), BF16), v((3, quarter, rank), BF16),
            v((rank, rank), BF16), v((rank, dim), BF16), v((3, rank, dim), BF16),
            v((rank, dim), BF16),
            v((2, quarter, rank), BF16), v((3, 2, quarter, rank), BF16),
            v((quarter, rank), BF16), v((nodes - 1, quarter, rank), BF16),
            v((nodes - 1, rank, dim), BF16), v((nrhs, rank), BF16), v((nrhs, rank), BF16),
            pltpu.SemaphoreType.DMA((copies,)), pltpu.SemaphoreType.DMA((copies,)),
            pltpu.SemaphoreType.DMA((10,)),
        ],
        compiler_params=pltpu.CompilerParams(
            collective_id=0, has_side_effects=True, vmem_limit_bytes=VMEM_MB * 1024 * 1024),
    )(*(pltpu.with_memory_space_constraint(x, pltpu.HBM) for x in (
        near, points, charges, bases, order, lift, nlift, zleaf, znode, ztop)))


def solution(mesh):
    n = mesh.shape["leaf"]

    def body(points, charges, order, near, bases, lift, nlift, zleaf, znode, ztop):
        return per_device(n, near, points, charges, order, bases, lift, nlift, zleaf, znode, ztop)

    return jax.shard_map(
        body, mesh=mesh, in_specs=(P("leaf", None),) * 10, out_specs=P("leaf", None), check_vma=False)
```

time: 63.1 us -> 47.6 us (0.75)
  the two profiles are of different devices: /device:TPU:5 before, /device:TPU:0 now
where the time goes in v2:
time: 47.6 us; the launch traced here: 47.1 us
  Pallas kernels  46.1 us (97%)
  local copies, waits for them, and re-layouts  0.97 us (2%)
    pallas_call x1, Pallas kernels, per_device(): pl.pallas_call(functools.partial(kernel, n), out_shape=jax.ShapeDtypeStru...  46.1 us
    unnamed x1, local copies, waits for them, and re-layouts  0.97 us

profile of v2, /device:TPU:0, one launch (start us, length us, event | category | flops | bytes accessed | tf_op | source)
XLA Modules:
  0.0 47.1 jit_solution(13344009055836647488)
XLA Ops:
  0.0 46.1 %shard_map.100 = bf16[2048,256]{1,0:T(8,128)(2,1)S(1)} custom-call(s32[1,2]{1,0:T(1,128)} %near_in.1, bf16[2048,128]{1,0:T(8,128)(2,1)} %points_in.1, bf16[2048,256]{1,0:T(8,128)(2,1)} %charges_in.1, bf16[2048,256]{1,0:T(8,128)(2,1)} %bases_in.1, s32[1,2048]{1,0:T(1,128)} %order_in.1, f32[256,256]{1,0:T(8,128)} %lift_in.1, f32[64,256]{1,0:T(8,128)} %nlift_in.1, ...), custom_call_target="tpu_custom_call" | custom-call | tf_op jit(solution)/shard_map/pallas_call | solution.py:446
  46.1 1.0 %copy.12 = bf16[2048,256]{1,0:T(8,128)(2,1)} copy(bf16[2048,256]{1,0:T(8,128)(2,1)S(1)} %shard_map.100) | data formatting | bytes 2097152

commit v3 on v2

--- a/solution.py
+++ b/solution.py
@@ -54,7 +54,7 @@
 
 def kernel(n, near_in, points_in, charges_in, bases_in, order_in, lift_in, nlift_in, zleaf_in, znode_in, ztop_in, out,
            near, points, charges, bases, order, lift, nlift, zleaf, znode, ztop, rhs, laug, raug, acc, acct,
-           p1, p2, p3, r1, r2, r3, rmask, prel,
+           p1, p2, p3, r1, r2, r3, rmask, prel, zrel,
            t1, t2, saug, racc, dsend, drecv, xsend, xrecv, fsend, frecv,
            c0, c0x, z0, z0x, ut, us, rs, nl, z1, z1s, z2, nv, nvs, c2, c2o, z2o, f1, f0,
            ssem, rsem, lsem):
@@ -72,8 +72,8 @@
     wide = leaf // PARTS
     half = PARTS // 2
     blocks = leaf // ROWS
-    gives = (me // 2 + me // 4) % 2 == 0
-    works = (me // 2 + me // 4) % 2 == 1
+    gives = (me // 2 + me // 4 + me // 8) % 2 == 0
+    works = (me // 2 + me // 4 + me // 8) % 2 == 1
 
     def flip(bits):
         where = me
@@ -88,7 +88,7 @@
     others = [(node + d) % nodes * 16 + part for d in range(1, nodes)]
 
     barrier = pltpu.get_barrier_semaphore()
-    partners = [flip(b) for b in (1, 2, 4, 6, 8, 12)] + others
+    partners = [flip(b) for b in (1, 2, 4, 6, 8, 10, 12)] + others
     for other in partners:
         pl.semaphore_signal(barrier, inc=1, device_id=(other,), device_id_type=MESH)
 
@@ -126,11 +126,12 @@
     step_rows = [pl.ds(j * step, step) for j in range(CHUNKS)]
 
     give_points = [link(points_in.at[r, :], p2.at[r, :], flip(2)) for r in part_rows[:half]]
-    give_detour = [link(points_in.at[r, :], prel.at[pl.ds(k * wide, wide), :], flip(4))
-                   for k, r in enumerate(part_rows[half:])]
-    detour_on = [link(prel.at[pl.ds(k * wide, wide), :], p2.at[r, :], flip(6))
-                 for k, r in enumerate(part_rows[half:])]
-    give_proxy = link(z0, z0x.at[1], flip(2))
+    detour_rows = [(pl.ds(half * wide + q * step, step), pl.ds(q * step, step)) for q in range(CHUNKS // 2)]
+    give_detour = [link(points_in.at[r, :], prel.at[at, :], flip((4, 10)[q % 2]))
+                   for q, (r, at) in enumerate(detour_rows)]
+    detour_on = [link(prel.at[at, :], p2.at[r, :], flip((6, 8)[q % 2])) for q, (r, at) in enumerate(detour_rows)]
+    give_proxy = link(z0, zrel, flip(10))
+    proxy_on = link(zrel, z0x.at[1], flip(8))
     give_coeff = link(c0, c0x.at[1], flip(2))
     give_rhs = [link(rhs.at[r, :], r2.at[r, :], flip(2)) for r in step_rows]
     share_points = [link(p2.at[r, :], p3.at[r, :], flip(1)) for r in part_rows]
@@ -194,6 +195,11 @@
 
     lax.fori_loop(0, PARTS, permute, 0)
 
+    @pl.when(gives)
+    def _():
+        arrive(give_detour[1::2] + [give_proxy])
+        start(detour_on[1::2] + [proxy_on])
+
     @pl.when(works)
     def _():
         enter(proxies_two + proxies_one + [mate_points])
@@ -261,12 +267,16 @@
         field1 = side + mm(field.astype(BF16), nl[...], 1, 1)
         f1[mine, :] = field1.astype(BF16)
 
-    def descend(far):
+    def descend(far, final):
         f0[...] = (far() + mm(f1[...], lift[...].astype(BF16), 1, 1)).astype(BF16)
 
         def body(block, carry):
             rows = pl.ds(pl.multiple_of(block * ROWS, ROWS), ROWS)
-            acc[rows, :] += mm(bases[rows, :], f0[...], 1, 1)
+            value = acc[rows, :] + mm(bases[rows, :], f0[...], 1, 1)
+            if final:
+                out[rows, :] = value.astype(BF16)
+            else:
+                acc[rows, :] = value
             return carry
 
         lax.fori_loop(0, blocks, body, 0)
@@ -286,8 +296,8 @@
         node_level()
         start(phase_two + give_rhs[2:4])
         own_tile(blocks // 2, blocks)
-        arrive(phase_b + [mate_points, mate_rhs])
-        start(top_proxies + [give_rhs[4]])
+        arrive([mate_points, mate_rhs])
+        start([give_rhs[4]])
 
         def mate(block, carry):
             rows = pl.ds(pl.multiple_of(block * ROWS, ROWS), ROWS)
@@ -305,22 +315,24 @@
             return carry
 
         lax.fori_loop(0, blocks, mate_tile, 0)
-        start([give_rhs[5], give_coeff])
+        start([give_rhs[5]])
+        arrive(phase_b)
+        start(top_proxies)
         arrive(phase_two)
         top_level()
         start(top_coeffs)
         arrive(top_proxies + top_coeffs)
         fields_down()
-        start([down_two, down_one] + give_rhs[6:])
+        start([down_two, down_one] + give_rhs[6:] + [give_coeff])
         arrive([down_two])
         start([down_rest])
         arrive([down_one, down_rest, back_far] + mate_far)
         descend(lambda: jnp.where(
-            near_one, frecv[...].astype(F32), mm(c0x[0], couple(z0x[0], z0[...]))))
+            near_one, frecv[...].astype(F32), mm(c0x[0], couple(z0x[0], z0[...]))), False)
         for k, copy in enumerate(back_part):
             copy.wait_recv()
             out[part_rows[k], :] = (acc[part_rows[k], :] + xrecv[k].astype(F32)).astype(BF16)
-        for copy in give_points + give_detour + [give_proxy, give_coeff] + give_rhs:
+        for copy in give_points + give_detour + detour_on[1::2] + [give_proxy, proxy_on, give_coeff] + give_rhs:
             copy.wait_send()
 
     @pl.when(works)
@@ -343,50 +355,56 @@
         def combine(k):
             xsend[k] = (racc[k % 2] + drecv[k].astype(F32)).astype(BF16)
 
-        arrive([give_points[0], mate_points, up_cross])
-        start([share_points[0]])
+        arrive([up_cross])
         carry_up()
         start([up_two])
         arrive([give_detour[0]])
         start([detour_on[0]])
+        arrive([give_points[0], mate_points])
+        start([share_points[0]])
+        arrive([give_detour[2]])
+        start([detour_on[2]])
         chosen(0)
         arrive([share_points[0]] + proxies_two)
         start(proxies_rest)
         diagonal(0)
         start([cross_part[0]])
-        arrive([give_points[1], give_detour[1]])
-        start([share_points[1], detour_on[1]])
-        chosen(1)
         arrive([cross_part[0]])
         combine(0)
         start([back_part[0]])
+        arrive([give_points[1]])
+        start([share_points[1]])
+        chosen(1)
         arrive([share_points[1]] + proxies_one + proxies_rest)
         start(phase_b)
         diagonal(1)
         start([cross_part[1]])
-        arrive([detour_on[0]])
+        arrive(detour_on[:2])
         start([share_points[2]])
         chosen(2)
-        arrive([cross_part[1], share_points[2], detour_on[1], up_near, up_two])
+        arrive([cross_part[1]])
+        combine(1)
+        start([back_part[1]])
+        arrive([share_points[2], up_near, up_two] + detour_on[2:])
         start([share_points[3]])
         node_level()
         start(phase_two)
-        combine(1)
         diagonal(2)
-        start([back_part[1], cross_part[2]])
-        arrive([share_points[3]] + phase_b)
-        start(top_proxies)
+        start([cross_part[2]])
+        arrive([share_points[3]])
         chosen(3)
-        arrive([cross_part[2]])
+        arrive([cross_part[2]] + phase_b)
         combine(2)
+        start([back_part[2]] + top_proxies)
         diagonal(3)
-        start([back_part[2], cross_part[3], mate_rhs])
-        arrive(phase_two + [give_proxy])
+        start([cross_part[3], mate_rhs])
+        arrive(phase_two + [proxy_on])
         top_level()
         fsend[...] = jnp.where(near_one, mm(c0[...], couple(z0[...], z0x[1])), 0.0).astype(BF16)
         start(top_coeffs + [back_far])
-        arrive(give_rhs[:3] + [cross_part[3]])
+        arrive(give_rhs[:3])
         start(share_rhs[:3])
+        arrive([cross_part[3]])
         combine(3)
         own_tile(0, blocks)
         arrive(top_proxies + top_coeffs + give_rhs[3:5])
@@ -404,28 +422,27 @@
             acct[...] = value if first == 0 else acct[...] + value
 
         def finish(j):
-            near_rhs, far_rhs = pick_rhs(step_rows[j])
-            return mm(t1[step_rows[j], :], near_rhs, 0, 0) + mm(t2[step_rows[j], :], far_rhs, 0, 0)
+            rows = step_rows[j]
+            arrive([give_rhs[j]])
+            start([share_rhs[j]])
+            acc[...] += mm(t1[rows, :], choose(r1[rows, :], r2[rows, :]), 0, 0)
+            arrive([share_rhs[j]])
+            acc[...] += mm(t2[rows, :], r3[rows, :], 0, 0)
 
         arrive(share_rhs[:4] + [mate_rhs])
         apply(0, 4)
-        arrive([give_rhs[5], down_two])
-        start([share_rhs[5], down_rest])
-        arrive([down_one, give_coeff, share_rhs[4], share_rhs[5]] + mate_far)
+        arrive([give_rhs[5]])
+        start([share_rhs[5]])
+        arrive([down_two, share_rhs[4], share_rhs[5]])
+        start([down_rest])
         apply(4, 6)
-        arrive([down_rest])
-        descend(lambda: mm(choose(c0x[1], c0x[0]), couple(choose(z0x[1], z0x[0]), z0[...])))
         for j in range(PARTS):
             acc[part_rows[j], :] += acct[:, j * wide:(j + 1) * wide].T
-        arrive([give_rhs[6]])
-        start([share_rhs[6]])
-        arrive([share_rhs[6]])
-        acc[...] += finish(6)
-        arrive([give_rhs[7]])
-        start([share_rhs[7]])
-        arrive([share_rhs[7]])
-        out[...] = (acc[...] + finish(7)).astype(BF16)
-        for copy in detour_on + share_points + share_rhs + cross_part + back_part + [back_far]:
+        finish(6)
+        finish(7)
+        arrive([down_one, down_rest, give_coeff] + mate_far)
+        descend(lambda: mm(choose(c0x[1], c0x[0]), couple(choose(z0x[1], z0x[0]), z0[...])), True)
+        for copy in detour_on[::2] + share_points + share_rhs + cross_part + back_part + [back_far]:
             copy.wait_send()
 
     for copy in (proxies_two + proxies_one + proxies_rest + mate_far + phase_b + phase_two + top_proxies + top_coeffs
@@ -456,7 +473,7 @@
             v((leaf, nrhs), F32), v((nrhs, leaf), F32),
             v((leaf, dim), BF16), v((leaf, dim), BF16), v((leaf, dim), BF16),
             v((leaf, nrhs), BF16), v((leaf, nrhs), BF16), v((leaf, nrhs), BF16), v((leaf, nrhs), BF16),
-            v((leaf // 2, dim), BF16),
+            v((leaf // 2, dim), BF16), v((rank, dim), BF16),
             v((leaf, leaf), BF16), v((leaf, leaf), BF16),
             v((2, wide, 2 * dim), BF16), v((2, wide, nrhs), F32),
             v((PARTS, wide, nrhs), BF16), v((PARTS, wide, nrhs), BF16),

time: 47.6 us -> 45.2 us (0.950)
  Pallas kernels: 46.1 us -> 44.1 us
    pallas_call x1, Pallas kernels: 46.1 us -> 44.1 us  [per_device(): pl.pallas_call(functools.partial(kernel, n), out_shape=jax.ShapeDtypeStru...]
where the time goes in v3:
time: 45.2 us; the launch traced here: 45.1 us
  Pallas kernels  44.1 us (98%)
  local copies, waits for them, and re-layouts  0.97 us (2%)
    pallas_call x1, Pallas kernels, per_device(): pl.pallas_call(functools.partial(kernel, n), out_shape=jax.ShapeDtypeStru...  44.1 us
    unnamed x1, local copies, waits for them, and re-layouts  0.97 us

profile of v3, /device:TPU:0, one launch (start us, length us, event | category | flops | bytes accessed | tf_op | source)
XLA Modules:
  0.0 45.1 jit_solution(12618623683090975045)
XLA Ops:
  0.0 44.1 %shard_map.100 = bf16[2048,256]{1,0:T(8,128)(2,1)S(1)} custom-call(s32[1,2]{1,0:T(1,128)} %near_in.1, bf16[2048,128]{1,0:T(8,128)(2,1)} %points_in.1, bf16[2048,256]{1,0:T(8,128)(2,1)} %charges_in.1, bf16[2048,256]{1,0:T(8,128)(2,1)} %bases_in.1, s32[1,2048]{1,0:T(1,128)} %order_in.1, f32[256,256]{1,0:T(8,128)} %lift_in.1, f32[64,256]{1,0:T(8,128)} %nlift_in.1, ...), custom_call_target="tpu_custom_call" | custom-call | tf_op jit(solution)/shard_map/pallas_call | solution.py:463
  44.1 1.0 %copy.12 = bf16[2048,256]{1,0:T(8,128)(2,1)} copy(bf16[2048,256]{1,0:T(8,128)(2,1)S(1)} %shard_map.100) | data formatting | bytes 2097152

commit v4 on v3

--- a/solution.py
+++ b/solution.py
@@ -54,7 +54,7 @@
 
 def kernel(n, near_in, points_in, charges_in, bases_in, order_in, lift_in, nlift_in, zleaf_in, znode_in, ztop_in, out,
            near, points, charges, bases, order, lift, nlift, zleaf, znode, ztop, rhs, laug, raug, acc, acct,
-           p1, p2, p3, r1, r2, r3, rmask, prel, zrel,
+           p1, p2, p3, r1, r2, r3, rmask, prel,
            t1, t2, saug, racc, dsend, drecv, xsend, xrecv, fsend, frecv,
            c0, c0x, z0, z0x, ut, us, rs, nl, z1, z1s, z2, nv, nvs, c2, c2o, z2o, f1, f0,
            ssem, rsem, lsem):
@@ -130,8 +130,7 @@
     give_detour = [link(points_in.at[r, :], prel.at[at, :], flip((4, 10)[q % 2]))
                    for q, (r, at) in enumerate(detour_rows)]
     detour_on = [link(prel.at[at, :], p2.at[r, :], flip((6, 8)[q % 2])) for q, (r, at) in enumerate(detour_rows)]
-    give_proxy = link(z0, zrel, flip(10))
-    proxy_on = link(zrel, z0x.at[1], flip(8))
+    give_proxy = link(z0, z0x.at[1], flip(2))
     give_coeff = link(c0, c0x.at[1], flip(2))
     give_rhs = [link(rhs.at[r, :], r2.at[r, :], flip(2)) for r in step_rows]
     share_points = [link(p2.at[r, :], p3.at[r, :], flip(1)) for r in part_rows]
@@ -195,11 +194,6 @@
 
     lax.fori_loop(0, PARTS, permute, 0)
 
-    @pl.when(gives)
-    def _():
-        arrive(give_detour[1::2] + [give_proxy])
-        start(detour_on[1::2] + [proxy_on])
-
     @pl.when(works)
     def _():
         enter(proxies_two + proxies_one + [mate_points])
@@ -288,6 +282,8 @@
         arrive([up_cross])
         carry_up()
         start([up_two, give_rhs[0], mate_rhs])
+        arrive(give_detour[1::2])
+        start(detour_on[1::2])
         arrive(proxies_two)
         start(proxies_rest + [give_rhs[1]])
         own_tile(0, blocks // 2)
@@ -315,7 +311,7 @@
             return carry
 
         lax.fori_loop(0, blocks, mate_tile, 0)
-        start([give_rhs[5]])
+        start(give_rhs[5:7])
         arrive(phase_b)
         start(top_proxies)
         arrive(phase_two)
@@ -323,7 +319,7 @@
         start(top_coeffs)
         arrive(top_proxies + top_coeffs)
         fields_down()
-        start([down_two, down_one] + give_rhs[6:] + [give_coeff])
+        start([down_two, down_one, give_rhs[7], give_coeff])
         arrive([down_two])
         start([down_rest])
         arrive([down_one, down_rest, back_far] + mate_far)
@@ -332,7 +328,7 @@
         for k, copy in enumerate(back_part):
             copy.wait_recv()
             out[part_rows[k], :] = (acc[part_rows[k], :] + xrecv[k].astype(F32)).astype(BF16)
-        for copy in give_points + give_detour + detour_on[1::2] + [give_proxy, proxy_on, give_coeff] + give_rhs:
+        for copy in give_points + give_detour + detour_on[1::2] + [give_proxy, give_coeff] + give_rhs:
             copy.wait_send()
 
     @pl.when(works)
@@ -398,7 +394,7 @@
         start([back_part[2]] + top_proxies)
         diagonal(3)
         start([cross_part[3], mate_rhs])
-        arrive(phase_two + [proxy_on])
+        arrive(phase_two + [give_proxy])
         top_level()
         fsend[...] = jnp.where(near_one, mm(c0[...], couple(z0[...], z0x[1])), 0.0).astype(BF16)
         start(top_coeffs + [back_far])
@@ -433,9 +429,10 @@
         apply(0, 4)
         arrive([give_rhs[5]])
         start([share_rhs[5]])
-        arrive([down_two, share_rhs[4], share_rhs[5]])
+        arrive(share_rhs[4:6])
+        apply(4, 6)
+        arrive([down_two])
         start([down_rest])
-        apply(4, 6)
         for j in range(PARTS):
             acc[part_rows[j], :] += acct[:, j * wide:(j + 1) * wide].T
         finish(6)
@@ -473,7 +470,7 @@
             v((leaf, nrhs), F32), v((nrhs, leaf), F32),
             v((leaf, dim), BF16), v((leaf, dim), BF16), v((leaf, dim), BF16),
             v((leaf, nrhs), BF16), v((leaf, nrhs), BF16), v((leaf, nrhs), BF16), v((leaf, nrhs), BF16),
-            v((leaf // 2, dim), BF16), v((rank, dim), BF16),
+            v((leaf // 2, dim), BF16),
             v((leaf, leaf), BF16), v((leaf, leaf), BF16),
             v((2, wide, 2 * dim), BF16), v((2, wide, nrhs), F32),
             v((PARTS, wide, nrhs), BF16), v((PARTS, wide, nrhs), BF16),

time: 45.2 us -> 45.2 us (level)
  no operation moved by 1% of the time
where the time goes in v4:
time: 45.2 us; the launch traced here: 45 us
  Pallas kernels  44 us (97%)
  local copies, waits for them, and re-layouts  0.97 us (2%)
    pallas_call x1, Pallas kernels, per_device(): pl.pallas_call(functools.partial(kernel, n), out_shape=jax.ShapeDtypeStru...  44 us
    unnamed x1, local copies, waits for them, and re-layouts  0.97 us

profile of v4, /device:TPU:0, one launch (start us, length us, event | category | flops | bytes accessed | tf_op | source)
XLA Modules:
  0.0 45.0 jit_solution(2680199048853158232)
XLA Ops:
  0.0 44.0 %shard_map.100 = bf16[2048,256]{1,0:T(8,128)(2,1)S(1)} custom-call(s32[1,2]{1,0:T(1,128)} %near_in.1, bf16[2048,128]{1,0:T(8,128)(2,1)} %points_in.1, bf16[2048,256]{1,0:T(8,128)(2,1)} %charges_in.1, bf16[2048,256]{1,0:T(8,128)(2,1)} %bases_in.1, s32[1,2048]{1,0:T(1,128)} %order_in.1, f32[256,256]{1,0:T(8,128)} %lift_in.1, f32[64,256]{1,0:T(8,128)} %nlift_in.1, ...), custom_call_target="tpu_custom_call" | custom-call | tf_op jit(solution)/shard_map/pallas_call | solution.py:460
  44.0 1.0 %copy.12 = bf16[2048,256]{1,0:T(8,128)(2,1)} copy(bf16[2048,256]{1,0:T(8,128)(2,1)S(1)} %shard_map.100) | data formatting | bytes 2097152
